TPU v7x, 32 devices: a whole 2x2x4 slice. The times are simulated.
32 devices in a mesh: dp: 8 (over z, core), expert: 4 (over y, x).
Axes of the slice: x: 2, y: 2, z: 4, core: 2. Of those that a mesh axis runs over, the one named last changes fastest.
Arguments:
- tokens: bfloat16 [24576, 2048], P(('dp', 'expert')), may hold values from -6 to 6
- target: bfloat16 [24576, 2048], P(('dp', 'expert')), may hold values from -4 to 4
- route_index: int32 [8, 4, 4, 16], P('dp', None, 'expert'), may hold values from 0 to 767, as said below
- route_count: int32 [8, 4, 4], P('dp', None, 'expert'), may hold values from 1 to 16, as said below
- route_gate: float32 [8, 4, 4, 16], P('dp', None, 'expert'), may hold values from 0.1 to 1
- gate_weight: bfloat16 [2048, 4, 768], P('dp', 'expert'), may hold values from -0.125 to 0.125
- up_weight: bfloat16 [2048, 4, 768], P('dp', 'expert'), may hold values from -0.125 to 0.125
- down_weight: bfloat16 [2048, 4, 768], P('dp', 'expert'), may hold values from -0.21875 to 0.21875
Outputs:
- token_grad: bfloat16 [24576, 2048], P(('dp', 'expert'))
- gate_gradient: float32 [2048, 4, 768], P('dp', 'expert')
- up_gradient: float32 [2048, 4, 768], P('dp', 'expert')
- down_gradient: float32 [2048, 4, 768], P('dp', 'expert')
Inputs may be any that keep to these rules, and one draw needn't show every extreme that they name: `route_index`: within each list of 16 slots the indices are distinct; each names a token of the source device. `route_count`: in every group one expert has all 16 slots live from every source device; slots at or beyond the count are unused.
All inputs are finite; a program needn't handle non-finite values.
Results may differ from a plain program's by a relative error of at most 0.0059.
Values may be sent and summed in bfloat16 or wider, within the bound.
A program may use at most 128 MiB of HBM per device.

v0:
```python
import jax
import jax.numpy as jnp
from jax import lax
from jax.sharding import PartitionSpec as P


def to_owners(block):
    return lax.all_to_all(block, "expert", split_axis=0, concat_axis=1, tiled=True)


def to_sources(block):
    return lax.all_to_all(block, "expert", split_axis=1, concat_axis=0, tiled=True)


def on_device(
    tokens, target, route_index, route_count, route_gate, gate_weight, up_weight, down_weight
):
    groups = lax.axis_size("dp")
    sources = lax.axis_size("expert")
    local_index = route_index[0, :, 0, :]
    live_count = route_count[0, :, 0]
    per_source = local_index.shape[1]
    model_width = tokens.shape[1]
    usable = jnp.arange(per_source, dtype=jnp.int32)[None, :] < live_count[:, None]
    slot_weight = jnp.where(usable, route_gate[0, :, 0, :], 0.0)
    outgoing = tokens[local_index] * usable[:, :, None].astype(tokens.dtype)
    expert_rows = to_owners(outgoing)
    full_gate, full_up, full_down = (
        lax.all_gather(gate_weight, "dp", axis=0, tiled=True),
        lax.all_gather(up_weight, "dp", axis=0, tiled=True),
        lax.all_gather(down_weight, "dp", axis=0, tiled=True),
    )
    gate_pre = jnp.einsum(
        "erd,def->erf", expert_rows, full_gate, preferred_element_type=jnp.float32
    )
    up_pre = jnp.einsum("erd,def->erf", expert_rows, full_up, preferred_element_type=jnp.float32)
    sigma = jax.nn.sigmoid(gate_pre)
    active = gate_pre * sigma
    hidden = (active * up_pre).astype(jnp.bfloat16)
    expert_out = jnp.einsum(
        "erf,def->erd", hidden, full_down, preferred_element_type=jnp.float32
    ).astype(jnp.bfloat16)
    returned = to_sources(expert_out)
    flat_index = local_index.reshape(-1)
    combined = (
        jnp.zeros((tokens.shape[0], model_width), jnp.float32)
        .at[flat_index]
        .add((slot_weight[:, :, None] * returned.astype(jnp.float32)).reshape(-1, model_width))
    )
    out_grad = combined - target.astype(jnp.float32)
    slot_grad = (slot_weight[:, :, None] * out_grad[local_index]).astype(jnp.bfloat16)
    owner_grad = to_owners(slot_grad)
    hidden_grad = jnp.einsum(
        "erd,def->erf", owner_grad, full_down, preferred_element_type=jnp.float32
    )
    gate_grad = (hidden_grad * up_pre * sigma * (1.0 + gate_pre * (1.0 - sigma))).astype(
        jnp.bfloat16
    )
    up_grad = (hidden_grad * active).astype(jnp.bfloat16)
    row_grad = (
        jnp.einsum("erf,def->erd", gate_grad, full_gate, preferred_element_type=jnp.float32)
        + jnp.einsum("erf,def->erd", up_grad, full_up, preferred_element_type=jnp.float32)
    ).astype(jnp.bfloat16)
    came_back = to_sources(row_grad)
    token_grad = (
        jnp.zeros((tokens.shape[0], model_width), jnp.float32)
        .at[flat_index]
        .add(came_back.astype(jnp.float32).reshape(-1, model_width))
        .astype(jnp.bfloat16)
    )
    factor = (groups * sources * per_source) ** (-0.5)
    rows_every, grad_every = (
        lax.all_to_all(expert_rows, "dp", split_axis=2, concat_axis=1, tiled=True),
        lax.all_to_all(owner_grad, "dp", split_axis=2, concat_axis=1, tiled=True),
    )
    hidden_piece = lax.all_gather(hidden, "dp", axis=1, tiled=True)
    gate_piece = lax.all_gather(gate_grad, "dp", axis=1, tiled=True)
    up_piece = lax.all_gather(up_grad, "dp", axis=1, tiled=True)
    gate_sum = jnp.einsum(
        "erd,erf->def", rows_every, gate_piece, preferred_element_type=jnp.float32
    )
    up_sum = jnp.einsum("erd,erf->def", rows_every, up_piece, preferred_element_type=jnp.float32)
    down_sum = jnp.einsum(
        "erd,erf->def", grad_every, hidden_piece, preferred_element_type=jnp.float32
    )
    gate_gradient = gate_sum * factor
    up_gradient = up_sum * factor
    down_gradient = down_sum * factor
    return (token_grad, gate_gradient, up_gradient, down_gradient)


def solution(mesh):
    return jax.shard_map(
        on_device,
        mesh=mesh,
        in_specs=(
            P(("dp", "expert"), None),
            P(("dp", "expert"), None),
            P("dp", None, "expert", None),
            P("dp", None, "expert"),
            P("dp", None, "expert", None),
            P("dp", "expert", None),
            P("dp", "expert", None),
            P("dp", "expert", None),
        ),
        out_specs=(
            P(("dp", "expert"), None),
            P("dp", "expert", None),
            P("dp", "expert", None),
            P("dp", "expert", None),
        ),
        check_vma=False,
    )
```

profile of v0, /device:TPU:0, one launch (start us, length us, event | category | flops | bytes accessed | tf_op | source)
XLA Modules:
  0.0 305.2 jit_solution(9919206521907058066)
XLA Ops:
  7.2 0.7 all-gather.7.cloned.1.call-update
  8.0 0.7 all-gather.9.cloned.1.call-update
  8.7 0.7 all-gather.11.cloned.1.call-update
  9.4 0.7 compare_select_fusion
  10.2 0.7 gather_fusion
  11.0 0.8 broadcast_multiply_fusion
  11.8 5.2 %all-to-all-start = ((bf16[4,16,2048]{2,1,0:T(8,128)(2,1)}), bf16[4,16,2048]{2,1,0:T(8,128)(2,1)S(1)}, u32[]{:S(2)}, u32[]{:S(2)}) async-start(bf16[4,16,2048]{2,1,0:T(8,128)(2,1)} %broadcast_multiply_fusion), calls=%async_computation | async-start | bytes 524288 | tf_op jit(solution)/shard_map/all_to_all | solution.py:8
  17.0 0.5 broadcast.132
  17.5 0.7 reduce.6
  18.3 4.1 %all-to-all-done = bf16[4,16,2048]{2,1,0:T(8,128)(2,1)S(1)} async-done(((bf16[4,16,2048]{2,1,0:T(8,128)(2,1)}), bf16[4,16,2048]{2,1,0:T(8,128)(2,1)S(1)}, u32[]{:S(2)}, u32[]{:S(2)}) %all-to-all-start) | async-done | bytes 262176 | tf_op jit(solution)/shard_map/all_to_all | solution.py:8
  22.4 1.9 copy.40
  24.3 0.5 broadcast.134
  24.9 13.3 %reduce.10 = bf16[2048,64]{1,0:T(8,128)(2,1)} reduce(bf16[2048,1,64]{2,1,0:T(2,128)(2,1)} %bitcast.114, bf16[]{:T(256)} %broadcast.134), dimensions={1}, to_apply=%bitcast.86.reduce_sub_computation | reduce | bytes 524290
  38.2 2.1 reshape.301
  40.3 4.9 %all-to-all-start.4 = ((bf16[8,2,8192]{2,1,0:T(2,128)(2,1)}), bf16[8,2,8192]{2,1,0:T(2,128)(2,1)}, u32[]{:S(2)}, u32[]{:S(2)}) async-start(bf16[8,2,8192]{2,1,0:T(2,128)(2,1)} %reshape.301), calls=%async_computation.4 | async-start | bytes 524288 | tf_op jit(solution)/shard_map/all_to_all | solution.py:73
  45.2 0.1 lt.53
  45.3 0.5 broadcast.133
  45.8 0.7 reduce.7
  46.6 8.4 %all-to-all-done.4 = bf16[8,2,8192]{2,1,0:T(2,128)(2,1)} async-done(((bf16[8,2,8192]{2,1,0:T(2,128)(2,1)}), bf16[8,2,8192]{2,1,0:T(2,128)(2,1)}, u32[]{:S(2)}, u32[]{:S(2)}) %all-to-all-start.4) | async-done | bytes 262176 | tf_op jit(solution)/shard_map/all_to_all | solution.py:73
  55.0 3.4 %reshape.302 = bf16[2048,1,64]{2,1,0:T(2,128)(2,1)} reshape(bf16[8,2,8192]{2,1,0:T(2,128)(2,1)} %all-to-all-done.4) | data formatting | bytes 524288
  58.4 3.4 %copy.41 = bf16[1,64,2048]{2,1,0:T(8,128)(2,1)} copy(bf16[1,64,2048]{1,0,2:T(2,128)(2,1)} %bitcast.112) | data formatting | bytes 524288 | tf_op jit(solution)/shard_map/all_to_all | solution.py:73
  61.8 1.7 copy.49
  63.5 3.2 %fusion.10 = f32[64,768]{1,0:T(8,128)} fusion(bf16[64,2048]{1,0:T(8,128)(2,1)S(1)} %bitcast.117, bf16[2048,1,768]{2,0,1:T(8,128)(2,1)} %all-gather.7.cloned.1.call-done), kind=kOutput, calls=%fused_computation.15 | convolution fusion | flops 201326592 | bytes 3604480 | tf_op jit(solution)/shard_map/erd,def->erf/dot_general | solution.py:33
  66.8 24.2 %all-gather.9.cloned.1.call-done = bf16[2048,1,768]{2,0,1:T(8,128)(2,1)} async-done(((bf16[256,1,768]{2,0,1:T(8,128)(2,1)}), bf16[2048,1,768]{2,0,1:T(8,128)(2,1)}) %all-gather.9.cloned.1.call-update) | async-done | bytes 3145744 | tf_op jit(solution)/shard_map/all_gather | solution.py:30
  90.9 3.2 %multiply_convert_fusion.3 = (bf16[64,768]{1,0:T(8,128)(2,1)S(1)}, f32[64,768]{1,0:T(8,128)}) fusion(f32[64,768]{1,0:T(8,128)} %fusion.10, bf16[64,2048]{1,0:T(8,128)(2,1)S(1)} %bitcast.118, bf16[2048,1,768]{2,0,1:T(8,128)(2,1)} %all-gather.9.cloned.1.call-done), kind=kOutput, calls=%fused_computation.44 | convolution fusion | flops 201621504 | bytes 3899392 | tf_op jit(solution)/shard_map/erd,def->erf/dot_general | solution.py:36
  94.1 35.6 %all-gather.11.cloned.1.call-done = bf16[2048,1,768]{2,0,1:T(8,128)(2,1)} async-done(((bf16[256,1,768]{2,0,1:T(8,128)(2,1)}), bf16[2048,1,768]{2,0,1:T(8,128)(2,1)}) %all-gather.11.cloned.1.call-update) | async-done | bytes 3145744 | tf_op jit(solution)/shard_map/all_gather | solution.py:31
  129.7 3.0 fusion.25
  132.7 1.2 copy.62
  133.9 3.8 %reduce.8 = bf16[64,2048]{1,0:T(8,128)(2,1)} reduce(bf16[64,1,2048]{2,1,0:T(2,128)(2,1)} %bitcast.123, bf16[]{:T(256)} %broadcast.134), dimensions={1}, to_apply=%bitcast.109.reduce_sub_computation | reduce | bytes 524290
  137.7 1.8 reshape.297
  139.5 4.2 %all-to-all-start.1 = ((bf16[4,2,16384]{2,1,0:T(2,128)(2,1)}), bf16[4,2,16384]{2,1,0:T(2,128)(2,1)}, u32[]{:S(2)}, u32[]{:S(2)}) async-start(bf16[4,2,16384]{2,1,0:T(2,128)(2,1)} %reshape.297), calls=%async_computation.1 | async-start | bytes 524288 | tf_op jit(solution)/shard_map/all_to_all | solution.py:12
  143.8 5.8 %all-to-all-done.1 = bf16[4,2,16384]{2,1,0:T(2,128)(2,1)} async-done(((bf16[4,2,16384]{2,1,0:T(2,128)(2,1)}), bf16[4,2,16384]{2,1,0:T(2,128)(2,1)}, u32[]{:S(2)}, u32[]{:S(2)}) %all-to-all-start.1) | async-done | bytes 262176 | tf_op jit(solution)/shard_map/all_to_all | solution.py:12
  149.7 1.9 reshape.298
  151.5 5.1 %scatter_custom_fusion = f32[768,2048]{1,0:T(8,128)} fusion(s32[64]{0:T(128)S(1)} %fusion.41, f32[]{:T(128)} %constant.5.clone.1, bf16[1,64,2048]{2,0,1:T(2,128)(2,1)} %bitcast.122, f32[64]{0:T(128)S(1)} %broadcast_select_fusion.1), kind=kCustom, calls=%fused_computation.19 | custom fusion | flops 393216 | bytes 6554116 | tf_op jit(solution)/shard_map/scatter-add | solution.py:48
  156.6 7.9 %convert_subtract_fusion = f32[768,2048]{1,0:T(8,128)} fusion(f32[768,2048]{1,0:T(8,128)} %scatter_custom_fusion, bf16[768,2048]{1,0:T(8,128)(2,1)} %param.9), kind=kLoop, calls=%fused_computation.4 | loop fusion | flops 3145728 | bytes 15728640 | tf_op jit(solution)/shard_map/sub | solution.py:50
  164.4 4.6 %gather_fusion.1 = f32[64,2048]{1,0:T(8,128)} fusion(f32[768,2048]{1,0:T(8,128)} %convert_subtract_fusion, s32[1024]{0:T(1024)S(1)} %pad_clamp_fusion), kind=kCustom, calls=%fused_computation.1 | custom fusion | bytes 1048832 | tf_op jit(solution)/shard_map/gather | solution.py:51
  169.0 1.8 multiply_convert_fusion
  170.8 4.1 %all-to-all-start.2 = ((bf16[4,16,2048]{2,1,0:T(8,128)(2,1)}), bf16[4,16,2048]{2,1,0:T(8,128)(2,1)}, u32[]{:S(2)}, u32[]{:S(2)}) async-start(bf16[4,16,2048]{2,1,0:T(8,128)(2,1)} %multiply_convert_fusion), calls=%async_computation.2 | async-start | bytes 524288 | tf_op jit(solution)/shard_map/all_to_all | solution.py:8
  174.9 16.5 %all-gather.2 = bf16[512,768]{1,0:T(8,128)(2,1)} all-gather(bf16[64,768]{1,0:T(8,128)(2,1)S(1)} %get-tuple-element.28), channel_id=4, replica_groups=mesh['dp'=8,'expert'=4] {'dp'}, dimensions={0}, use_global_device_ids=true | all-gather | bytes 884736 | tf_op jit(solution)/shard_map/all_gather | solution.py:76
  191.4 2.8 multiply_convert_fusion.2
  194.2 0.2 copy-done.2
  194.4 1.1 fusion.4
  195.5 1.1 fusion.28
  196.5 1.2 copy.61
  197.7 3.8 %reduce.9 = bf16[64,2048]{1,0:T(8,128)(2,1)} reduce(bf16[64,1,2048]{2,1,0:T(2,128)(2,1)} %bitcast.124, bf16[]{:T(256)} %broadcast.134), dimensions={1}, to_apply=%bitcast.108.reduce_sub_computation | reduce | bytes 524290
  201.5 1.9 reshape.299
  203.4 4.2 %all-to-all-start.3 = ((bf16[4,2,16384]{2,1,0:T(2,128)(2,1)}), bf16[4,2,16384]{2,1,0:T(2,128)(2,1)}, u32[]{:S(2)}, u32[]{:S(2)}) async-start(bf16[4,2,16384]{2,1,0:T(2,128)(2,1)} %reshape.299), calls=%async_computation.3 | async-start | bytes 524288 | tf_op jit(solution)/shard_map/all_to_all | solution.py:12
  207.6 16.5 %all-gather = bf16[512,768]{1,0:T(8,128)(2,1)S(1)} all-gather(bf16[64,768]{1,0:T(8,128)(2,1)} %copy-done.4), channel_id=2, replica_groups=mesh['dp'=8,'expert'=4] {'dp'}, dimensions={0}, use_global_device_ids=true | all-gather | bytes 884736 | tf_op jit(solution)/shard_map/all_gather | solution.py:77
  224.1 1.3 fusion.33
  225.4 3.0 copy.46
  228.4 3.4 %copy.43 = bf16[1,64,2048]{1,0,2:T(2,128)(2,1)} copy(bf16[1,64,2048]{2,1,0:T(8,128)(2,1)} %bitcast.22) | data formatting | bytes 524288 | tf_op jit(solution)/shard_map/all_to_all | solution.py:8
  231.8 13.3 %reduce.11 = bf16[2048,64]{1,0:T(8,128)(2,1)} reduce(bf16[2048,1,64]{2,1,0:T(2,128)(2,1)} %bitcast.115, bf16[]{:T(256)} %broadcast.134), dimensions={1}, to_apply=%bitcast.88.reduce_sub_computation | reduce | bytes 524290
  245.1 2.1 reshape.303
  247.3 4.1 %all-to-all-start.5 = ((bf16[8,2,8192]{2,1,0:T(2,128)(2,1)}), bf16[8,2,8192]{2,1,0:T(2,128)(2,1)}, u32[]{:S(2)}, u32[]{:S(2)}) async-start(bf16[8,2,8192]{2,1,0:T(2,128)(2,1)} %reshape.303), calls=%async_computation.5 | async-start | bytes 524288 | tf_op jit(solution)/shard_map/all_to_all | solution.py:74
  251.3 19.9 %all-gather.1 = bf16[512,768]{1,0:T(8,128)(2,1)S(1)} all-gather(bf16[64,768]{1,0:T(8,128)(2,1)S(1)} %get-tuple-element.25), channel_id=3, replica_groups=mesh['dp'=8,'expert'=4] {'dp'}, dimensions={0}, use_global_device_ids=true | all-gather | bytes 884736 | tf_op jit(solution)/shard_map/all_gather | solution.py:78
  271.3 1.3 fusion.32
  272.6 3.0 copy.47
  275.6 1.9 reshape.300
  277.5 5.1 %scatter_custom_fusion.1 = f32[768,2048]{1,0:T(8,128)} fusion(s32[64]{0:T(128)S(1)} %fusion.41, f32[]{:T(128)} %constant.5.clone.1, bf16[1,64,2048]{2,0,1:T(2,128)(2,1)} %bitcast.125), kind=kCustom, calls=%fused_computation.17 | custom fusion | flops 262144 | bytes 6553604 | tf_op jit(solution)/shard_map/scatter-add | solution.py:68
  282.5 4.9 %convert_element_type.75 = bf16[768,2048]{1,0:T(8,128)(2,1)} convert(f32[768,2048]{1,0:T(8,128)} %scatter_custom_fusion.1) | non-fusion elementwise | flops 1572864 | bytes 9437184 | tf_op jit(solution)/shard_map/convert_element_type | solution.py:69
  287.5 3.4 %reshape.304 = bf16[2048,1,64]{2,1,0:T(2,128)(2,1)} reshape(bf16[8,2,8192]{2,1,0:T(2,128)(2,1)} %all-to-all-done.5) | data formatting | bytes 524288
  290.8 2.3 copy.44
  293.3 2.4 fusion.31
  295.7 3.0 copy.48
  (35 shorter events, 0.8 us)
Async XLA Ops:
  7.2 3.0 copy-start
  7.2 10.4 %copy-start.5 = (s32[1,4,1,16]{3,2,1,0:T(1,128)S(1)}, s32[1,4,1,16]{3,2,1,0:T(1,128)}, u32[]{:S(2)}) copy-start(s32[1,4,1,16]{3,2,1,0:T(1,128)} %param.10) | copy-start | bytes 772
  7.2 3.8 %copy-start.7 = (s32[1,4,1]{1,2,0:T(1,128)S(1)}, s32[1,4,1]{1,2,0:T(1,128)}, u32[]{:S(2)}) copy-start(s32[1,4,1]{1,2,0:T(1,128)} %param.11) | copy-start | bytes 52
  7.2 56.3 %all-gather.7.cloned.1.call-start = ((), (), s32[]{:S(2)}) async-start(), calls=%async_computation.6 | async-start | bytes 3538944 | tf_op jit(solution)/shard_map/all_gather | solution.py:29
  7.9 83.0 %all-gather.9.cloned.1.call-start = ((), (), s32[]{:S(2)}) async-start(), calls=%async_computation.7 | async-start | bytes 3538944 | tf_op jit(solution)/shard_map/all_gather | solution.py:30
  8.7 121.0 %all-gather.11.cloned.1.call-start = ((), (), s32[]{:S(2)}) async-start(), calls=%async_computation.8 | async-start | bytes 3538944 | tf_op jit(solution)/shard_map/all_gather | solution.py:31
  10.9 34.9 %copy-start.6 = (f32[1,4,1,16]{3,2,1,0:T(1,128)S(1)}, f32[1,4,1,16]{3,2,1,0:T(1,128)}, u32[]{:S(2)}) copy-start(f32[1,4,1,16]{3,2,1,0:T(1,128)} %param.12) | copy-start | bytes 772
  11.8 10.6 %all-to-all-start = ((bf16[4,16,2048]{2,1,0:T(8,128)(2,1)}), bf16[4,16,2048]{2,1,0:T(8,128)(2,1)S(1)}, u32[]{:S(2)}, u32[]{:S(2)}) async-start(bf16[4,16,2048]{2,1,0:T(8,128)(2,1)} %broadcast_multiply_fusion), calls=%async_computation | async-start | bytes 524288 | tf_op jit(solution)/shard_map/all_to_all | solution.py:8
  40.3 14.7 %all-to-all-start.4 = ((bf16[8,2,8192]{2,1,0:T(2,128)(2,1)}), bf16[8,2,8192]{2,1,0:T(2,128)(2,1)}, u32[]{:S(2)}, u32[]{:S(2)}) async-start(bf16[8,2,8192]{2,1,0:T(2,128)(2,1)} %reshape.301), calls=%async_computation.4 | async-start | bytes 524288 | tf_op jit(solution)/shard_map/all_to_all | solution.py:73
  94.1 49.6 %copy-start.3 = (bf16[8,8,8,256]{3,2,1,0:T(8,128)(2,1)S(1)}, bf16[8,8,8,256]{3,2,1,0:T(8,128)(2,1)}, u32[]{:S(2)}) copy-start(bf16[8,8,8,256]{3,2,1,0:T(8,128)(2,1)} %copy.49) | copy-start | bytes 786436
  139.5 10.2 %all-to-all-start.1 = ((bf16[4,2,16384]{2,1,0:T(2,128)(2,1)}), bf16[4,2,16384]{2,1,0:T(2,128)(2,1)}, u32[]{:S(2)}, u32[]{:S(2)}) async-start(bf16[4,2,16384]{2,1,0:T(2,128)(2,1)} %reshape.297), calls=%async_computation.1 | async-start | bytes 524288 | tf_op jit(solution)/shard_map/all_to_all | solution.py:12
  170.8 20.5 %all-to-all-start.2 = ((bf16[4,16,2048]{2,1,0:T(8,128)(2,1)}), bf16[4,16,2048]{2,1,0:T(8,128)(2,1)}, u32[]{:S(2)}, u32[]{:S(2)}) async-start(bf16[4,16,2048]{2,1,0:T(8,128)(2,1)} %multiply_convert_fusion), calls=%async_computation.2 | async-start | bytes 524288 | tf_op jit(solution)/shard_map/all_to_all | solution.py:8
  191.4 3.0 copy-start.2
  191.4 4.1 %copy-start.1 = (bf16[2048,1,768]{2,0,1:T(8,128)(2,1)S(1)}, bf16[2048,1,768]{2,0,1:T(8,128)(2,1)}, u32[]{:S(2)}) copy-start(bf16[2048,1,768]{2,0,1:T(8,128)(2,1)} %all-gather.7.cloned.1.call-done) | copy-start | bytes 9437188
  194.2 2.3 copy-start.4
  203.4 43.9 %all-to-all-start.3 = ((bf16[4,2,16384]{2,1,0:T(2,128)(2,1)}), bf16[4,2,16384]{2,1,0:T(2,128)(2,1)}, u32[]{:S(2)}, u32[]{:S(2)}) async-start(bf16[4,2,16384]{2,1,0:T(2,128)(2,1)} %reshape.299), calls=%async_computation.3 | async-start | bytes 524288 | tf_op jit(solution)/shard_map/all_to_all | solution.py:12
  247.3 40.2 %all-to-all-start.5 = ((bf16[8,2,8192]{2,1,0:T(2,128)(2,1)}), bf16[8,2,8192]{2,1,0:T(2,128)(2,1)}, u32[]{:S(2)}, u32[]{:S(2)}) async-start(bf16[8,2,8192]{2,1,0:T(2,128)(2,1)} %reshape.303), calls=%async_computation.5 | async-start | bytes 524288 | tf_op jit(solution)/shard_map/all_to_all | solution.py:74
Sparse Core Ops, SparseCore 0:
  9.6 40.9 all-gather.6
  52.3 38.6 all-gather.8
  92.6 37.1 all-gather.10
where the time goes:
time: 307 us; the launch traced here: 305 us
  waiting for transfers between devices  80.1 us (26%)
  other arithmetic  62 us (20%)
  blocking collectives  52.9 us (17%)
  local copies, waits for them, and re-layouts  50.3 us (16%)
  starting transfers between devices  26.7 us (9%)
  matrix products  19.3 us (6%)
  between operations  13.9 us (5%)
    all_gather x1, waiting for transfers between devices, on_device(): lax.all_gather(down_weight, 'dp', axis=0, tiled=True)  35.6 us
    unnamed x6, other arithmetic  35.6 us
    unnamed x32, local copies, waits for them, and re-layouts  31.1 us
    all_gather x1, waiting for transfers between devices, on_device(): lax.all_gather(up_weight, 'dp', axis=0, tiled=True)  24.2 us
    all_gather x1, blocking collectives, on_device(): up_piece = lax.all_gather(up_grad, 'dp', axis=1, tiled=True)  19.9 us
    all_gather x1, blocking collectives, on_device(): gate_piece = lax.all_gather(gate_grad, 'dp', axis=1, tiled=True)  16.5 us
    all_gather x1, blocking collectives, on_device(): hidden_piece = lax.all_gather(hidden, 'dp', axis=1, tiled=True)  16.5 us
    all_to_all x2, starting transfers between devices, to_owners(): lax.all_to_all(block, 'expert', split_axis=0, concat_axis=1, tiled=True)  9.24 us
  transfers between devices with their start and end apart: 9, of which 5 were waited for; matrix products, arithmetic and copies ran while one was open for 25% of the time, Pallas kernels for 0%

commit v1 on v0

--- a/solution.py
+++ b/solution.py
@@ -2,6 +2,22 @@
 import jax.numpy as jnp
 from jax import lax
 from jax.sharding import PartitionSpec as P
+
+
+def summed_both_ways(x, axis, dim, product):
+    size, index, rows = (lax.axis_size(axis), lax.axis_index(axis), x.shape[dim])
+    upward = [(i, (i + 1) % size) for i in range(size)]
+    behind = [(i, (i - 1) % size) for i in range(size)]
+    half = size // 2
+    from_left = from_right = x
+    total = product(x, index * rows)
+    for hop in range(1, half + 1):
+        from_left = lax.ppermute(from_left, axis, upward)
+        if hop < size - half:
+            from_right = lax.ppermute(from_right, axis, behind)
+            total = total + product(from_right, (index + hop) % size * rows)
+        total = total + product(from_left, (index - hop) % size * rows)
+    return total
 
 
 def to_owners(block):
@@ -75,11 +91,20 @@
     )
     hidden_piece = lax.all_gather(hidden, "dp", axis=1, tiled=True)
     gate_piece = lax.all_gather(gate_grad, "dp", axis=1, tiled=True)
-    up_piece = lax.all_gather(up_grad, "dp", axis=1, tiled=True)
     gate_sum = jnp.einsum(
         "erd,erf->def", rows_every, gate_piece, preferred_element_type=jnp.float32
     )
-    up_sum = jnp.einsum("erd,erf->def", rows_every, up_piece, preferred_element_type=jnp.float32)
+    up_sum = summed_both_ways(
+        up_grad,
+        "dp",
+        1,
+        lambda shard, at: jnp.einsum(
+            "erd,erf->def",
+            lax.dynamic_slice_in_dim(rows_every, at, shard.shape[1], axis=1),
+            shard,
+            preferred_element_type=jnp.float32,
+        ),
+    )
     down_sum = jnp.einsum(
         "erd,erf->def", grad_every, hidden_piece, preferred_element_type=jnp.float32
     )

time: 307 us -> 292 us (0.951)
  waiting for transfers between devices: 80.1 us -> 102 us
  local copies, waits for them, and re-layouts: 50.3 us -> 29.5 us
  blocking collectives: 52.9 us -> 32.8 us
  starting transfers between devices: 26.7 us -> 36.3 us
  other arithmetic: 62 us -> 53.7 us
    all_gather x1 -> x0, blocking collectives: 19.9 us -> none  [on_device(): up_piece = lax.all_gather(up_grad, 'dp', axis=1, tiled=True)]
    unnamed x32 -> x36, local copies, waits for them, and re-layouts: 31.1 us -> 16.8 us
    all_gather x1, waiting for transfers between devices: 24.2 us -> 36 us  [on_device(): lax.all_gather(up_weight, 'dp', axis=0, tiled=True)]
    ppermute x0 -> x7, starting transfers between devices: none -> 10.8 us  [the longest x3 9.62 us: summed_both_ways(): from_right = lax.ppermute(from_right, axis, behind)]
    unnamed x6, other arithmetic: 35.6 us -> 28.6 us
    ppermute x0 -> x7, waiting for transfers between devices: none -> 6.21 us  [the longest x4 5.32 us: summed_both_ways(): from_left = lax.ppermute(from_left, axis, upward)]
    dot_general x1 -> x8, matrix products: 1.29 us -> 4.97 us  [on_device(): jnp.einsum('erd,erf->def', lax.dynamic_slice_in_dim(rows_every, at, shard...]
    all_to_all x1, waiting for transfers between devices: 8.38 us -> 12 us  [on_device(): lax.all_to_all(expert_rows, 'dp', split_axis=2, concat_axis=1, tiled=True)]
  transfers between devices with their start and end apart: 9 -> 16, of which waited for: 5 -> 8; matrix products, arithmetic and copies ran while one was open for 25% -> 23% of each run, Pallas kernels for 0% -> 0%
where the time goes in v1:
time: 292 us; the launch traced here: 291 us
  waiting for transfers between devices  102 us (35%)
  other arithmetic  53.7 us (18%)
  starting transfers between devices  36.3 us (12%)
  blocking collectives  32.8 us (11%)
  local copies, waits for them, and re-layouts  29.5 us (10%)
  matrix products  22.3 us (8%)
  between operations  14.2 us (5%)
    all_gather x1, waiting for transfers between devices, on_device(): lax.all_gather(up_weight, 'dp', axis=0, tiled=True)  36 us
    all_gather x1, waiting for transfers between devices, on_device(): lax.all_gather(down_weight, 'dp', axis=0, tiled=True)  35.6 us
    unnamed x6, other arithmetic  28.6 us
    unnamed x36, local copies, waits for them, and re-layouts  16.8 us
    all_gather x1, blocking collectives, on_device(): hidden_piece = lax.all_gather(hidden, 'dp', axis=1, tiled=True)  16.5 us
    all_gather x1, blocking collectives, on_device(): gate_piece = lax.all_gather(gate_grad, 'dp', axis=1, tiled=True)  16.4 us
    all_to_all x1, waiting for transfers between devices, on_device(): lax.all_to_all(expert_rows, 'dp', split_axis=2, concat_axis=1, tiled=True)  12 us
    ppermute x3, starting transfers between devices, summed_both_ways(): from_right = lax.ppermute(from_right, axis, behind)  9.62 us
  transfers between devices with their start and end apart: 16, of which 8 were waited for; matrix products, arithmetic and copies ran while one was open for 23% of the time, Pallas kernels for 0%

profile of v1, /device:TPU:0, one launch (start us, length us, event | category | flops | bytes accessed | tf_op | source)
XLA Modules:
  0.0 290.5 jit_solution(14955747990581886196)
XLA Ops:
  7.2 0.7 all-gather.6.cloned.1.call-update
  8.0 0.7 all-gather.8.cloned.1.call-update
  8.7 0.7 all-gather.10.cloned.1.call-update
  9.4 0.7 compare_select_fusion
  10.2 0.7 gather_fusion
  11.0 0.8 broadcast_multiply_fusion
  11.8 5.2 %all-to-all-start = ((bf16[4,16,2048]{2,1,0:T(8,128)(2,1)}), bf16[4,16,2048]{2,1,0:T(8,128)(2,1)S(1)}, u32[]{:S(2)}, u32[]{:S(2)}) async-start(bf16[4,16,2048]{2,1,0:T(8,128)(2,1)} %broadcast_multiply_fusion), calls=%async_computation | async-start | bytes 524288 | tf_op jit(solution)/shard_map/all_to_all | solution.py:24
  17.5 0.7 reduce.6
  18.3 4.1 %all-to-all-done = bf16[4,16,2048]{2,1,0:T(8,128)(2,1)S(1)} async-done(((bf16[4,16,2048]{2,1,0:T(8,128)(2,1)}), bf16[4,16,2048]{2,1,0:T(8,128)(2,1)S(1)}, u32[]{:S(2)}, u32[]{:S(2)}) %all-to-all-start) | async-done | bytes 262176 | tf_op jit(solution)/shard_map/all_to_all | solution.py:24
  22.4 0.7 copy.42
  23.1 0.5 broadcast.145
  23.7 11.5 %reduce.10 = bf16[2048,64]{1,0:T(8,128)(2,1)S(1)} reduce(bf16[2048,1,64]{2,1,0:T(2,128)(2,1)S(1)} %bitcast.160, bf16[]{:T(256)} %broadcast.145), dimensions={1}, to_apply=%bitcast.133.reduce_sub_computation | reduce | bytes 524290
  35.2 1.1 reshape.369
  36.3 4.9 %all-to-all-start.4 = ((bf16[8,2,8192]{2,1,0:T(2,128)(2,1)}), bf16[8,2,8192]{2,1,0:T(2,128)(2,1)S(1)}, u32[]{:S(2)}, u32[]{:S(2)}) async-start(bf16[8,2,8192]{2,1,0:T(2,128)(2,1)} %reshape.369), calls=%async_computation.4 | async-start | bytes 524288 | tf_op jit(solution)/shard_map/all_to_all | solution.py:89
  41.4 0.5 broadcast.144
  41.9 0.7 reduce.7
  42.7 12.0 %all-to-all-done.4 = bf16[8,2,8192]{2,1,0:T(2,128)(2,1)S(1)} async-done(((bf16[8,2,8192]{2,1,0:T(2,128)(2,1)}), bf16[8,2,8192]{2,1,0:T(2,128)(2,1)S(1)}, u32[]{:S(2)}, u32[]{:S(2)}) %all-to-all-start.4) | async-done | bytes 262176 | tf_op jit(solution)/shard_map/all_to_all | solution.py:89
  54.7 0.6 reshape.370
  55.3 0.6 copy.43
  56.0 2.5 fusion.10
  58.6 36.0 %all-gather.8.cloned.1.call-done = bf16[2048,1,768]{2,0,1:T(8,128)(2,1)} async-done(((bf16[256,1,768]{2,0,1:T(8,128)(2,1)}), bf16[2048,1,768]{2,0,1:T(8,128)(2,1)}) %all-gather.8.cloned.1.call-update) | async-done | bytes 3145744 | tf_op jit(solution)/shard_map/all_gather | solution.py:46
  94.6 3.2 %multiply_convert_fusion.3 = (bf16[64,768]{1,0:T(8,128)(2,1)S(1)}, f32[64,768]{1,0:T(8,128)}) fusion(f32[64,768]{1,0:T(8,128)S(1)} %fusion.10, bf16[64,2048]{1,0:T(8,128)(2,1)S(1)} %bitcast.164, bf16[2048,1,768]{2,0,1:T(8,128)(2,1)} %all-gather.8.cloned.1.call-done), kind=kOutput, calls=%fused_computation.51 | convolution fusion | flops 201621504 | bytes 3899392 | tf_op jit(solution)/shard_map/erd,def->erf/dot_general | solution.py:52
  97.8 35.6 %all-gather.10.cloned.1.call-done = bf16[2048,1,768]{2,0,1:T(8,128)(2,1)} async-done(((bf16[256,1,768]{2,0,1:T(8,128)(2,1)}), bf16[2048,1,768]{2,0,1:T(8,128)(2,1)}) %all-gather.10.cloned.1.call-update) | async-done | bytes 3145744 | tf_op jit(solution)/shard_map/all_gather | solution.py:47
  133.4 2.9 %fusion.25 = bf16[1,64,2048]{2,1,0:T(8,128)(2,1)S(1)} fusion(bf16[64,768]{1,0:T(8,128)(2,1)S(1)} %get-tuple-element.28, bf16[2048,1,768]{2,0,1:T(8,128)(2,1)} %all-gather.10.cloned.1.call-done), kind=kOutput, calls=%fused_computation.24 | convolution fusion | flops 201457664 | bytes 3506176 | tf_op jit(solution)/shard_map/erf,def->erd/dot_general | solution.py:56
  136.8 2.1 reduce.8
  138.9 0.9 reshape.365
  139.8 3.6 %all-to-all-start.1 = ((bf16[4,2,16384]{2,1,0:T(2,128)(2,1)}), bf16[4,2,16384]{2,1,0:T(2,128)(2,1)S(1)}, u32[]{:S(2)}, u32[]{:S(2)}) async-start(bf16[4,2,16384]{2,1,0:T(2,128)(2,1)} %reshape.365), calls=%async_computation.1 | async-start | bytes 524288 | tf_op jit(solution)/shard_map/all_to_all | solution.py:28
  143.5 5.7 %all-to-all-done.1 = bf16[4,2,16384]{2,1,0:T(2,128)(2,1)S(1)} async-done(((bf16[4,2,16384]{2,1,0:T(2,128)(2,1)}), bf16[4,2,16384]{2,1,0:T(2,128)(2,1)S(1)}, u32[]{:S(2)}, u32[]{:S(2)}) %all-to-all-start.1) | async-done | bytes 262176 | tf_op jit(solution)/shard_map/all_to_all | solution.py:28
  149.2 1.0 reshape.366
  150.1 5.3 %scatter_custom_fusion = f32[768,2048]{1,0:T(8,128)} fusion(s32[64]{0:T(128)S(1)} %fusion.78, f32[]{:T(128)} %constant.57.clone.1, bf16[1,64,2048]{2,0,1:T(2,128)(2,1)} %bitcast.175, f32[64]{0:T(128)S(1)} %broadcast_select_fusion.1), kind=kCustom, calls=%fused_computation.19 | custom fusion | flops 393216 | bytes 6554116 | tf_op jit(solution)/shard_map/scatter-add | solution.py:64
  155.4 6.9 %convert_subtract_fusion = f32[768,2048]{1,0:T(8,128)} fusion(f32[768,2048]{1,0:T(8,128)} %scatter_custom_fusion, bf16[768,2048]{1,0:T(8,128)(2,1)S(1)} %copy-done.5), kind=kLoop, calls=%fused_computation.4 | loop fusion | flops 3145728 | bytes 15728640 | tf_op jit(solution)/shard_map/sub | solution.py:66
  162.3 4.7 %gather_fusion.1 = f32[64,2048]{1,0:T(8,128)} fusion(f32[768,2048]{1,0:T(8,128)} %convert_subtract_fusion, s32[1024]{0:T(1024)S(1)} %pad_clamp_fusion), kind=kCustom, calls=%fused_computation.1 | custom fusion | bytes 1048832 | tf_op jit(solution)/shard_map/gather | solution.py:67
  167.0 1.8 multiply_convert_fusion
  168.9 4.1 %all-to-all-start.2 = ((bf16[4,16,2048]{2,1,0:T(8,128)(2,1)}), bf16[4,16,2048]{2,1,0:T(8,128)(2,1)}, u32[]{:S(2)}, u32[]{:S(2)}) async-start(bf16[4,16,2048]{2,1,0:T(8,128)(2,1)} %multiply_convert_fusion), calls=%async_computation.2 | async-start | bytes 524288 | tf_op jit(solution)/shard_map/all_to_all | solution.py:24
  172.9 16.5 %all-gather.1 = bf16[512,768]{1,0:T(8,128)(2,1)} all-gather(bf16[64,768]{1,0:T(8,128)(2,1)S(1)} %get-tuple-element.28), channel_id=3, replica_groups=mesh['dp'=8,'expert'=4] {'dp'}, dimensions={0}, use_global_device_ids=true | all-gather | bytes 884736 | tf_op jit(solution)/shard_map/all_gather | solution.py:92
  189.4 1.8 multiply_convert_fusion.2
  191.6 3.2 %collective-permute-start = (bf16[1,64,768]{2,1,0:T(8,128)(2,1)S(1)}, bf16[1,64,768]{2,1,0:T(8,128)(2,1)}, u32[]{:S(2)}, u32[]{:S(2)}) collective-permute-start(bf16[1,64,768]{2,1,0:T(8,128)(2,1)S(1)} %bitcast.186), channel_id=1, source_target_pairs={{0,28},{4,0},{8,4},{12,8},{16,12},{20,16},{24,20},{28,24},{1,29},{... | collective-permute-start | bytes 294920 | tf_op jit(solution)/shard_map/ppermute | solution.py:17
  194.8 16.4 %all-gather = bf16[512,768]{1,0:T(8,128)(2,1)} all-gather(bf16[64,768]{1,0:T(8,128)(2,1)S(1)} %get-tuple-element.24), channel_id=2, replica_groups=mesh['dp'=8,'expert'=4] {'dp'}, dimensions={0}, use_global_device_ids=true | all-gather | bytes 884736 | tf_op jit(solution)/shard_map/all_gather | solution.py:93
  211.1 2.9 %fusion.4 = f32[64,2048]{1,0:T(8,128)S(1)} fusion(bf16[64,768]{1,0:T(8,128)(2,1)S(1)} %get-tuple-element.25, bf16[2048,1,768]{2,0,1:T(8,128)(2,1)} %all-gather.8.cloned.1.call-done), kind=kOutput, calls=%fused_computation.9 | convolution fusion | flops 201326592 | bytes 3768320 | tf_op jit(solution)/shard_map/erf,def->erd/dot_general | solution.py:78
  214.1 1.1 fusion.28
  215.6 2.1 reduce.9
  217.7 0.9 reshape.367
  218.6 4.3 %all-to-all-start.3 = ((bf16[4,2,16384]{2,1,0:T(2,128)(2,1)}), bf16[4,2,16384]{2,1,0:T(2,128)(2,1)}, u32[]{:S(2)}, u32[]{:S(2)}) async-start(bf16[4,2,16384]{2,1,0:T(2,128)(2,1)} %reshape.367), calls=%async_computation.3 | async-start | bytes 524288 | tf_op jit(solution)/shard_map/all_to_all | solution.py:28
  223.6 1.7 copy.49
  225.3 2.2 copy.46
  227.5 11.5 %reduce.11 = bf16[2048,64]{1,0:T(8,128)(2,1)S(1)} reduce(bf16[2048,1,64]{2,1,0:T(2,128)(2,1)S(1)} %bitcast.161, bf16[]{:T(256)} %broadcast.145), dimensions={1}, to_apply=%bitcast.135.reduce_sub_computation | reduce | bytes 524290
  239.0 1.1 reshape.371
  240.5 3.2 %collective-permute-start.2 = (bf16[1,64,768]{2,1,0:T(8,128)(2,1)}, bf16[1,64,768]{2,1,0:T(8,128)(2,1)S(1)}, u32[]{:S(2)}, u32[]{:S(2)}) collective-permute-start(bf16[1,64,768]{2,1,0:T(8,128)(2,1)} %collective-permute-done), channel_id=1, source_target_pairs={{0,28},{4,0},{8,4},{12,8},{16,12},{20,16},{24,20},{28,24},{1,29},{... | collective-permute-start | bytes 294920 | tf_op jit(solution)/shard_map/ppermute | solution.py:17
  243.7 1.2 convolution_add_fusion.4
  244.9 1.2 convolution_add_fusion.3
  246.1 3.4 %all-to-all-start.5 = ((bf16[8,2,8192]{2,1,0:T(2,128)(2,1)}), bf16[8,2,8192]{2,1,0:T(2,128)(2,1)S(1)}, u32[]{:S(2)}, u32[]{:S(2)}) async-start(bf16[8,2,8192]{2,1,0:T(2,128)(2,1)} %reshape.371), calls=%async_computation.5 | async-start | bytes 524288 | tf_op jit(solution)/shard_map/all_to_all | solution.py:90
  249.5 1.2 reshape.368
  250.7 4.6 %scatter_custom_fusion.1 = f32[768,2048]{1,0:T(8,128)} fusion(s32[64]{0:T(128)S(1)} %fusion.78, f32[]{:T(128)} %constant.57.clone.1, bf16[1,64,2048]{2,0,1:T(2,128)(2,1)S(1)} %bitcast.178), kind=kCustom, calls=%fused_computation.17 | custom fusion | flops 262144 | bytes 6815748 | tf_op jit(solution)/shard_map/scatter-add | solution.py:84
  255.3 4.9 %convert_element_type.75 = bf16[768,2048]{1,0:T(8,128)(2,1)} convert(f32[768,2048]{1,0:T(8,128)} %scatter_custom_fusion.1) | non-fusion elementwise | flops 1572864 | bytes 9437184 | tf_op jit(solution)/shard_map/convert_element_type | solution.py:85
  260.6 1.2 fusion.48
  261.8 3.2 %collective-permute-start.4 = (bf16[1,64,768]{2,1,0:T(8,128)(2,1)S(1)}, bf16[1,64,768]{2,1,0:T(8,128)(2,1)S(1)}, u32[]{:S(2)}, u32[]{:S(2)}) collective-permute-start(bf16[1,64,768]{2,1,0:T(8,128)(2,1)S(1)} %collective-permute-done.2), channel_id=1, source_target_pairs={{0,28},{4,0},{8,4},{12,8},{16,12},{20,16},{24,20},{28,24},{1,29},{... | collective-permute-start | bytes 294920 | tf_op jit(solution)/shard_map/ppermute | solution.py:17
  265.3 0.9 collective-permute-done.5
  266.5 0.9 collective-permute-done.4
  267.7 4.4 %collective-permute-done.6 = bf16[1,64,768]{2,1,0:T(8,128)(2,1)S(1)} collective-permute-done((bf16[1,64,768]{2,1,0:T(8,128)(2,1)S(1)}, bf16[1,64,768]{2,1,0:T(8,128)(2,1)S(1)}, u32[]{:S(2)}, u32[]{:S(2)}) %collective-permute-start.6) | collective-permute-done | bytes 98336 | tf_op jit(solution)/shard_map/ppermute | solution.py:15
  272.4 1.7 copy.50
  274.1 1.9 reshape.372
  276.0 2.4 copy.47
  278.6 2.4 fusion.31
  281.0 3.0 %copy.51 = f32[256,1,768]{2,1,0:T(1,128)} copy(f32[256,1,768]{0,2,1:T(8,128)} %fusion.31) | data formatting | bytes 1572864
  (59 shorter events, 5.2 us)
Async XLA Ops:
  7.2 3.0 %copy-start = (bf16[768,2048]{1,0:T(8,128)(2,1)S(1)}, bf16[768,2048]{1,0:T(8,128)(2,1)}, u32[]{:S(2)}) copy-start(bf16[768,2048]{1,0:T(8,128)(2,1)} %param.8) | copy-start | bytes 9437188
  7.2 10.4 %copy-start.7 = (s32[1,4,1,16]{3,2,1,0:T(1,128)S(1)}, s32[1,4,1,16]{3,2,1,0:T(1,128)}, u32[]{:S(2)}) copy-start(s32[1,4,1,16]{3,2,1,0:T(1,128)} %param.10) | copy-start | bytes 772
  7.2 3.8 %copy-start.9 = (s32[1,4,1]{1,2,0:T(1,128)S(1)}, s32[1,4,1]{1,2,0:T(1,128)}, u32[]{:S(2)}) copy-start(s32[1,4,1]{1,2,0:T(1,128)} %param.11) | copy-start | bytes 52
  7.2 48.8 %all-gather.6.cloned.1.call-start = ((), (), s32[]{:S(2)}) async-start(), calls=%async_computation.6 | async-start | bytes 3538944 | tf_op jit(solution)/shard_map/all_gather | solution.py:45
  7.9 86.7 %all-gather.8.cloned.1.call-start = ((), (), s32[]{:S(2)}) async-start(), calls=%async_computation.7 | async-start | bytes 3538944 | tf_op jit(solution)/shard_map/all_gather | solution.py:46
  8.7 124.7 %all-gather.10.cloned.1.call-start = ((), (), s32[]{:S(2)}) async-start(), calls=%async_computation.8 | async-start | bytes 3538944 | tf_op jit(solution)/shard_map/all_gather | solution.py:47
  10.9 30.9 %copy-start.8 = (f32[1,4,1,16]{3,2,1,0:T(1,128)S(1)}, f32[1,4,1,16]{3,2,1,0:T(1,128)}, u32[]{:S(2)}) copy-start(f32[1,4,1,16]{3,2,1,0:T(1,128)} %param.12) | copy-start | bytes 772
  11.8 10.6 %all-to-all-start = ((bf16[4,16,2048]{2,1,0:T(8,128)(2,1)}), bf16[4,16,2048]{2,1,0:T(8,128)(2,1)S(1)}, u32[]{:S(2)}, u32[]{:S(2)}) async-start(bf16[4,16,2048]{2,1,0:T(8,128)(2,1)} %broadcast_multiply_fusion), calls=%async_computation | async-start | bytes 524288 | tf_op jit(solution)/shard_map/all_to_all | solution.py:24
  36.3 18.4 %all-to-all-start.4 = ((bf16[8,2,8192]{2,1,0:T(2,128)(2,1)}), bf16[8,2,8192]{2,1,0:T(2,128)(2,1)S(1)}, u32[]{:S(2)}, u32[]{:S(2)}) async-start(bf16[8,2,8192]{2,1,0:T(2,128)(2,1)} %reshape.369), calls=%async_computation.4 | async-start | bytes 524288 | tf_op jit(solution)/shard_map/all_to_all | solution.py:89
  58.6 74.8 %copy-start.6 = (f32[64,768]{1,0:T(8,128)}, f32[64,768]{1,0:T(8,128)S(1)}, u32[]{:S(2)}) copy-start(f32[64,768]{1,0:T(8,128)S(1)} %fusion.10) | copy-start | bytes 589828
  139.8 9.4 %all-to-all-start.1 = ((bf16[4,2,16384]{2,1,0:T(2,128)(2,1)}), bf16[4,2,16384]{2,1,0:T(2,128)(2,1)S(1)}, u32[]{:S(2)}, u32[]{:S(2)}) async-start(bf16[4,2,16384]{2,1,0:T(2,128)(2,1)} %reshape.365), calls=%async_computation.1 | async-start | bytes 524288 | tf_op jit(solution)/shard_map/all_to_all | solution.py:28
  150.1 5.3 %copy-start.5 = (bf16[768,2048]{1,0:T(8,128)(2,1)S(1)}, bf16[768,2048]{1,0:T(8,128)(2,1)}, u32[]{:S(2)}) copy-start(bf16[768,2048]{1,0:T(8,128)(2,1)} %param.9) | copy-start | bytes 9437188
  162.3 27.1 %copy-start.3 = (bf16[2048,1,768]{2,0,1:T(8,128)(2,1)S(1)}, bf16[2048,1,768]{2,0,1:T(8,128)(2,1)}, u32[]{:S(2)}) copy-start(bf16[2048,1,768]{2,0,1:T(8,128)(2,1)} %all-gather.10.cloned.1.call-done) | copy-start | bytes 9437188
  168.9 20.5 %all-to-all-start.2 = ((bf16[4,16,2048]{2,1,0:T(8,128)(2,1)}), bf16[4,16,2048]{2,1,0:T(8,128)(2,1)}, u32[]{:S(2)}, u32[]{:S(2)}) async-start(bf16[4,16,2048]{2,1,0:T(8,128)(2,1)} %multiply_convert_fusion), calls=%async_computation.2 | async-start | bytes 524288 | tf_op jit(solution)/shard_map/all_to_all | solution.py:24
  191.2 22.9 %copy-start.2 = (bf16[2048,1,768]{2,0,1:T(8,128)(2,1)S(1)}, bf16[2048,1,768]{2,0,1:T(8,128)(2,1)}, u32[]{:S(2)}) copy-start(bf16[2048,1,768]{2,0,1:T(8,128)(2,1)} %all-gather.6.cloned.1.call-done) | copy-start | bytes 9437188
  191.2 48.9 %collective-permute-start.1 = (bf16[1,64,768]{2,1,0:T(8,128)(2,1)S(1)}, bf16[1,64,768]{2,1,0:T(8,128)(2,1)}, u32[]{:S(2)}, u32[]{:S(2)}) collective-permute-start(bf16[1,64,768]{2,1,0:T(8,128)(2,1)S(1)} %bitcast.185), channel_id=1, source_target_pairs={{0,4},{4,8},{8,12},{12,16},{16,20},{20,24},{24,28},{28,0},{1,5},{5... | collective-permute-start | bytes 294920 | tf_op jit(solution)/shard_map/ppermute | solution.py:15
  191.6 48.9 %collective-permute-start = (bf16[1,64,768]{2,1,0:T(8,128)(2,1)S(1)}, bf16[1,64,768]{2,1,0:T(8,128)(2,1)}, u32[]{:S(2)}, u32[]{:S(2)}) collective-permute-start(bf16[1,64,768]{2,1,0:T(8,128)(2,1)S(1)} %bitcast.186), channel_id=1, source_target_pairs={{0,28},{4,0},{8,4},{12,8},{16,12},{20,16},{24,20},{28,24},{1,29},{... | collective-permute-start | bytes 294920 | tf_op jit(solution)/shard_map/ppermute | solution.py:17
  215.2 8.0 %copy-start.4 = (bf16[512,768]{1,0:T(8,128)(2,1)S(1)}, bf16[512,768]{1,0:T(8,128)(2,1)}, u32[]{:S(2)}) copy-start(bf16[512,768]{1,0:T(8,128)(2,1)} %all-gather) | copy-start | bytes 2359300
  218.6 27.5 %all-to-all-start.3 = ((bf16[4,2,16384]{2,1,0:T(2,128)(2,1)}), bf16[4,2,16384]{2,1,0:T(2,128)(2,1)}, u32[]{:S(2)}, u32[]{:S(2)}) async-start(bf16[4,2,16384]{2,1,0:T(2,128)(2,1)} %reshape.367), calls=%async_computation.3 | async-start | bytes 524288 | tf_op jit(solution)/shard_map/all_to_all | solution.py:28
  240.1 20.1 %collective-permute-start.3 = (bf16[1,64,768]{2,1,0:T(8,128)(2,1)}, bf16[1,64,768]{2,1,0:T(8,128)(2,1)}, u32[]{:S(2)}, u32[]{:S(2)}) collective-permute-start(bf16[1,64,768]{2,1,0:T(8,128)(2,1)} %collective-permute-done.1), channel_id=1, source_target_pairs={{0,4},{4,8},{8,12},{12,16},{16,20},{20,24},{24,28},{28,0},{1,5},{5... | collective-permute-start | bytes 294920 | tf_op jit(solution)/shard_map/ppermute | solution.py:15
  240.5 21.3 %collective-permute-start.2 = (bf16[1,64,768]{2,1,0:T(8,128)(2,1)}, bf16[1,64,768]{2,1,0:T(8,128)(2,1)S(1)}, u32[]{:S(2)}, u32[]{:S(2)}) collective-permute-start(bf16[1,64,768]{2,1,0:T(8,128)(2,1)} %collective-permute-done), channel_id=1, source_target_pairs={{0,28},{4,0},{8,4},{12,8},{16,12},{20,16},{24,20},{28,24},{1,29},{... | collective-permute-start | bytes 294920 | tf_op jit(solution)/shard_map/ppermute | solution.py:17
  246.1 28.0 %all-to-all-start.5 = ((bf16[8,2,8192]{2,1,0:T(2,128)(2,1)}), bf16[8,2,8192]{2,1,0:T(2,128)(2,1)S(1)}, u32[]{:S(2)}, u32[]{:S(2)}) async-start(bf16[8,2,8192]{2,1,0:T(2,128)(2,1)} %reshape.371), calls=%async_computation.5 | async-start | bytes 524288 | tf_op jit(solution)/shard_map/all_to_all | solution.py:90
  260.2 6.1 %collective-permute-start.5 = (bf16[1,64,768]{2,1,0:T(8,128)(2,1)}, bf16[1,64,768]{2,1,0:T(8,128)(2,1)S(1)}, u32[]{:S(2)}, u32[]{:S(2)}) collective-permute-start(bf16[1,64,768]{2,1,0:T(8,128)(2,1)} %collective-permute-done.3), channel_id=1, source_target_pairs={{0,4},{4,8},{8,12},{12,16},{16,20},{20,24},{24,28},{28,0},{1,5},{5... | collective-permute-start | bytes 294920 | tf_op jit(solution)/shard_map/ppermute | solution.py:15
  261.8 5.6 %collective-permute-start.4 = (bf16[1,64,768]{2,1,0:T(8,128)(2,1)S(1)}, bf16[1,64,768]{2,1,0:T(8,128)(2,1)S(1)}, u32[]{:S(2)}, u32[]{:S(2)}) collective-permute-start(bf16[1,64,768]{2,1,0:T(8,128)(2,1)S(1)} %collective-permute-done.2), channel_id=1, source_target_pairs={{0,28},{4,0},{8,4},{12,8},{16,12},{20,16},{24,20},{28,24},{1,29},{... | collective-permute-start | bytes 294920 | tf_op jit(solution)/shard_map/ppermute | solution.py:17
  266.2 5.8 %collective-permute-start.6 = (bf16[1,64,768]{2,1,0:T(8,128)(2,1)S(1)}, bf16[1,64,768]{2,1,0:T(8,128)(2,1)S(1)}, u32[]{:S(2)}, u32[]{:S(2)}) collective-permute-start(bf16[1,64,768]{2,1,0:T(8,128)(2,1)S(1)} %collective-permute-done.5), channel_id=1, source_target_pairs={{0,4},{4,8},{8,12},{12,16},{16,20},{20,24},{24,28},{28,0},{1,5},{5... | collective-permute-start | bytes 294920 | tf_op jit(solution)/shard_map/ppermute | solution.py:15
  276.0 8.0 %copy-start.1 = (bf16[768,2048]{1,0:T(8,128)(2,1)S(1)}, bf16[768,2048]{1,0:T(8,128)(2,1)}, u32[]{:S(2)}) copy-start(bf16[768,2048]{1,0:T(8,128)(2,1)} %param.8) | copy-start | bytes 9437188
Sparse Core Ops, SparseCore 0:
  9.7 44.6 all-gather.5
  56.0 38.5 all-gather.7
  96.2 37.1 all-gather.9
